TPU v7x, 256 devices: a whole 4x4x8 slice. The times are simulated.
256 devices in a mesh: feat: 4 (over y), node: 64 (over x, z, core).
Axes of the slice: x: 4, y: 4, z: 8, core: 2. Of those that a mesh axis runs over, the one named last changes fastest.
Arguments:
- features: bfloat16 [64, 768, 2048], P('node', 'feat'), may hold values from -6 to 6
- tiles: bfloat16 [64, 48, 128, 128], P('node'), may hold values from -0.3125 to 0.3125
- tile_rows: int32 [64, 48], P('node'), may hold values from 0 to 15, as said below
- tile_cols: int32 [64, 48], P('node'), may hold values from 0 to 31
- send_rows: int32 [64, 64, 32], P('node'), may hold values from 0 to 2047, as said below
- send_count: int32 [64, 64], P('node'), may hold values from 0 to 32, as said below
- w_neigh: bfloat16 [768, 1024], P('feat'), may hold values from -0.15625 to 0.15625
- w_self: bfloat16 [768, 1024], P('feat'), may hold values from -0.15625 to 0.15625
- cotangent: bfloat16 [64, 2048, 1024], P('node', 'feat'), may hold values from -16 to 16
Outputs:
- hidden: bfloat16 [64, 2048, 1024], P('node', 'feat')
- grad_features: bfloat16 [64, 768, 2048], P('node', 'feat')
- grad_neigh: float32 [768, 1024], P('feat')
- grad_self: float32 [768, 1024], P('feat')
Inputs may be any that keep to these rules, and one draw needn't show every extreme that they name: `tile_rows`: for each partition the first 16 tiles feed the row blocks 0, 1, 2 and so on in order, so that every block of rows has a tile. `send_rows`: rows may repeat within a list. `send_count`: A partition sends nothing to itself, and every partition fills all 32 slots toward at least one other partition.
All inputs are finite; a program needn't handle non-finite values.
Results may differ from a plain program's by a relative error of at most 0.0058.
Values may be sent and summed in bfloat16 or wider, within the bound.
A program may use at most 128 MiB of HBM per device.

v0:
```python
import jax
import jax.numpy as jnp
from jax import lax
from jax.sharding import PartitionSpec as P


def per_device(
    features, tiles, tile_rows, tile_cols, send_rows, send_count, w_neigh, w_self, cotangent
):
    own_cols = features[0]
    feat_dev, own_rows = own_cols.shape
    tile_vals = tiles[0]
    tile_side = tile_vals.shape[1]
    row_ids = tile_rows[0]
    col_ids = tile_cols[0]
    targets = send_rows[0]
    amounts = send_count[0]
    parts, slots = targets.shape
    live_slots = lax.broadcasted_iota(jnp.int32, (parts, slots), 1) < amounts[:, None]
    picked = jnp.take(own_cols, targets.reshape(-1), axis=1).reshape(feat_dev, parts, slots)
    picked = jnp.where(live_slots[None], picked, jnp.zeros((), own_cols.dtype))
    arrived = lax.all_to_all(picked, "node", split_axis=1, concat_axis=1, tiled=True)
    extended = jnp.concatenate([own_cols, arrived.reshape(feat_dev, parts * slots)], axis=1)
    col_blocks = extended.shape[1] // tile_side
    row_blocks = own_rows // tile_side
    gathered_cols = extended.reshape(feat_dev, col_blocks, tile_side)[:, col_ids, :]
    partial_sums = jnp.einsum(
        "fkj,kij->fki", gathered_cols, tile_vals, preferred_element_type=jnp.float32
    )
    row_onehot = (row_ids[:, None] == lax.broadcasted_iota(jnp.int32, (1, row_blocks), 1)).astype(
        jnp.float32
    )
    aggregated = jnp.einsum(
        "fki,kr->fri", partial_sums, row_onehot, precision=lax.Precision.HIGHEST
    )
    aggregated = aggregated.reshape(feat_dev, own_rows).astype(jnp.bfloat16)
    full_neigh, full_self = (
        lax.all_gather(w_neigh, "feat", axis=0, tiled=True),
        lax.all_gather(w_self, "feat", axis=0, tiled=True),
    )
    agg_rows, self_rows = (
        lax.all_to_all(aggregated, "feat", split_axis=1, concat_axis=0, tiled=True),
        lax.all_to_all(own_cols, "feat", split_axis=1, concat_axis=0, tiled=True),
    )
    first_dims = (((0,), (0,)), ((), ()))
    preact = lax.dot_general(agg_rows, full_neigh, first_dims, preferred_element_type=jnp.float32)
    preact = preact + lax.dot_general(
        self_rows, full_self, first_dims, preferred_element_type=jnp.float32
    )
    hidden = jax.nn.silu(preact).astype(jnp.bfloat16)
    gate_sig = jax.nn.sigmoid(preact)
    grad_pre = (
        cotangent[0].astype(jnp.float32) * gate_sig * (1.0 + preact * (1.0 - gate_sig))
    ).astype(jnp.bfloat16)
    grad_scale = float(own_rows * lax.axis_size("node")) ** (-0.5)
    last_dims = (((1,), (1,)), ((), ()))
    term_neigh = jnp.dot(agg_rows, grad_pre, preferred_element_type=jnp.float32)
    term_self = jnp.dot(self_rows, grad_pre, preferred_element_type=jnp.float32)
    share_neigh, share_self = (
        lax.psum_scatter(term_neigh, "feat", scatter_dimension=0, tiled=True),
        lax.psum_scatter(term_self, "feat", scatter_dimension=0, tiled=True),
    )
    total_neigh, total_self = lax.psum((share_neigh, share_self), "node")
    back_agg = lax.dot_general(
        full_neigh, grad_pre, last_dims, preferred_element_type=jnp.float32
    ).astype(jnp.bfloat16)
    back_self = lax.dot_general(
        full_self, grad_pre, last_dims, preferred_element_type=jnp.float32
    ).astype(jnp.bfloat16)
    grad_agg, grad_own = (
        lax.all_to_all(back_agg, "feat", split_axis=0, concat_axis=1, tiled=True),
        lax.all_to_all(back_self, "feat", split_axis=0, concat_axis=1, tiled=True),
    )
    grad_blocks = grad_agg.reshape(feat_dev, row_blocks, tile_side)[:, row_ids, :]
    spread = jnp.einsum("fki,kij->fkj", grad_blocks, tile_vals, preferred_element_type=jnp.float32)
    col_onehot = (col_ids[:, None] == lax.broadcasted_iota(jnp.int32, (1, col_blocks), 1)).astype(
        jnp.float32
    )
    grad_ext = jnp.einsum("fkj,kc->fcj", spread, col_onehot, precision=lax.Precision.HIGHEST)
    grad_ext = grad_ext.reshape(feat_dev, col_blocks * tile_side)
    outgoing = grad_ext[:, own_rows:].reshape(feat_dev, parts, slots)
    returned = lax.all_to_all(outgoing, "node", split_axis=1, concat_axis=1, tiled=True)
    returned = jnp.where(live_slots[None], returned, jnp.zeros((), returned.dtype))
    grad_cols = grad_ext[:, :own_rows] + grad_own.astype(jnp.float32)
    grad_cols = grad_cols.at[:, targets.reshape(-1)].add(returned.reshape(feat_dev, parts * slots))
    return (
        hidden[None],
        grad_cols.astype(jnp.bfloat16)[None],
        total_neigh * grad_scale,
        total_self * grad_scale,
    )


def solution(mesh):
    placed = (
        P("node", "feat", None),
        P("node", None, None, None),
        P("node", None),
        P("node", None),
        P("node", None, None),
        P("node", None),
        P("feat", None),
        P("feat", None),
        P("node", "feat", None),
    )
    return jax.shard_map(
        per_device,
        mesh=mesh,
        in_specs=placed,
        out_specs=(
            P("node", "feat", None),
            P("node", "feat", None),
            P("feat", None),
            P("feat", None),
        ),
        check_vma=False,
    )
```

profile of v0, /device:TPU:8, one launch (start us, length us, event | category | flops | bytes accessed | tf_op | source)
XLA Modules:
  0.0 419.9 jit_solution(5458794064605959569)
XLA Ops:
  7.2 0.0 all-gather.3.cloned.1.call-start
  7.2 0.7 all-gather.3.cloned.1.call-update
  7.9 0.8 copy.54
  8.7 0.7 compare_and_fusion
  9.4 0.1 reshape_squeeze.7
  9.5 1.4 copy.53
  11.0 0.1 copy.52
  11.1 9.1 %gather_fusion = bf16[2048,192]{1,0:T(8,128)(2,1)} fusion(bf16[192,2048]{0,1:T(8,128)(2,1)S(1)} %bitcast.96, s32[2048]{0:T(1024)S(1)} %broadcast_clamp_fusion), kind=kCustom, calls=%fused_computation | custom fusion | bytes 1581056 | tf_op jit(solution)/shard_map/jit(_take)/gather | solution.py:20
  20.2 0.1 iota_compare_fusion
  20.3 3.4 select_select_fusion
  23.7 11.9 %all-to-all-start = ((bf16[192,64,32]{0,2,1:T(8,128)(2,1)}), bf16[192,64,32]{0,2,1:T(8,128)(2,1)S(1)}, u32[]{:S(2)}, u32[]{:S(2)}) async-start(bf16[192,64,32]{0,2,1:T(8,128)(2,1)} %select_select_fusion), calls=%async_computation | async-start | bytes 2097152 | tf_op jit(solution)/shard_map/all_to_all | solution.py:22
  35.7 0.0 all-gather.5.cloned.1.call-start
  35.7 0.7 all-gather.5.cloned.1.call-update
  36.4 0.2 copy.72
  36.6 1.1 copy.55
  37.7 26.1 %all-to-all-done = bf16[192,64,32]{0,2,1:T(8,128)(2,1)S(1)} async-done(((bf16[192,64,32]{0,2,1:T(8,128)(2,1)}), bf16[192,64,32]{0,2,1:T(8,128)(2,1)S(1)}, u32[]{:S(2)}, u32[]{:S(2)}) %all-to-all-start) | async-done | bytes 786464 | tf_op jit(solution)/shard_map/all_to_all | solution.py:22
  63.8 1.2 copy.56
  65.1 1.5 pad_maximum_fusion
  66.6 2.4 gather_fusion.1
  69.0 2.8 fusion.8
  71.8 5.2 %fusion.26 = bf16[192,16,128]{2,1,0:T(8,128)(2,1)} fusion(f32[192,48,128]{2,0,1:T(8,128)S(1)} %fusion.8, s32[48]{0:T(128)S(1)} %bitcast.112), kind=kOutput, calls=%fused_computation.32 | convolution fusion | flops 226886400 | bytes 5505216 | tf_op jit(solution)/shard_map/fki,kr->fri/dot_general | solution.py:33
  77.0 1.8 convert_element_type.50
  78.9 1.0 copy.58
  79.9 4.9 %all-to-all-start.1 = ((bf16[192,4,512]{2,0,1:T(8,128)(2,1)}), bf16[192,4,512]{2,0,1:T(8,128)(2,1)S(1)}, u32[]{:S(2)}, u32[]{:S(2)}) async-start(bf16[192,4,512]{2,0,1:T(8,128)(2,1)} %copy.58), calls=%async_computation.1 | async-start | bytes 1572864 | tf_op jit(solution)/shard_map/all_to_all | solution.py:42
  84.8 1.4 all_to_all.58
  86.2 2.2 copy.59
  88.4 7.8 %all-to-all-done.1 = bf16[192,4,512]{2,0,1:T(8,128)(2,1)S(1)} async-done(((bf16[192,4,512]{2,0,1:T(8,128)(2,1)}), bf16[192,4,512]{2,0,1:T(8,128)(2,1)S(1)}, u32[]{:S(2)}, u32[]{:S(2)}) %all-to-all-start.1) | async-done | bytes 786464 | tf_op jit(solution)/shard_map/all_to_all | solution.py:42
  96.2 4.9 %all-to-all-start.2 = ((bf16[192,4,512]{2,0,1:T(8,128)(2,1)}), bf16[192,4,512]{2,0,1:T(8,128)(2,1)S(1)}, u32[]{:S(2)}, u32[]{:S(2)}) async-start(bf16[192,4,512]{2,0,1:T(8,128)(2,1)} %copy.59), calls=%async_computation.2 | async-start | bytes 1572864 | tf_op jit(solution)/shard_map/all_to_all | solution.py:43
  101.1 3.8 fusion.39
  104.9 6.8 %all-to-all-done.2 = bf16[192,4,512]{2,0,1:T(8,128)(2,1)S(1)} async-done(((bf16[192,4,512]{2,0,1:T(8,128)(2,1)}), bf16[192,4,512]{2,0,1:T(8,128)(2,1)S(1)}, u32[]{:S(2)}, u32[]{:S(2)}) %all-to-all-start.2) | async-done | bytes 786464 | tf_op jit(solution)/shard_map/all_to_all | solution.py:43
  111.7 5.1 %fusion.15 = (bf16[512,1024]{1,0:T(8,128)(2,1)S(1)}, bf16[1,512,1024]{2,1,0:T(8,128)(2,1)}) fusion(bf16[1,512,1024]{2,1,0:T(8,128)(2,1)} %param.17, f32[512,1024]{1,0:T(8,128)} %fusion.39, bf16[768,512]{1,0:T(8,128)(2,1)S(1)} %bitcast.103, bf16[768,1024]{1,0:T(8,128)(2,1)} %all-gather.5.cloned.1.call-done), kind=kOutput, calls=%fused_computation.17 | convolution fusion | flops 812122112 | bytes 7602176 | tf_op jit(solution)/shard_map/dot_general | solution.py:47
  116.8 1.0 copy-done.3
  117.9 2.7 fusion.40
  120.5 0.0 reduce-scatter.5.cloned.1.call-start
  120.6 1.1 copy-done.4
  121.7 2.7 convolution_bitcast_fusion
  124.5 2.4 fusion.24
  126.9 1.2 copy.60
  128.1 4.9 %all-to-all-start.3 = ((bf16[4,192,512]{2,1,0:T(8,128)(2,1)}), bf16[4,192,512]{2,1,0:T(8,128)(2,1)S(1)}, u32[]{:S(2)}, u32[]{:S(2)}) async-start(bf16[4,192,512]{2,1,0:T(8,128)(2,1)} %bitcast.108), calls=%async_computation.3 | async-start | bytes 1572864 | tf_op jit(solution)/shard_map/all_to_all | solution.py:71
  133.0 3.3 fusion.25
  136.4 2.3 copy.65
  138.7 14.1 %all-to-all-done.3 = bf16[4,192,512]{2,1,0:T(8,128)(2,1)S(1)} async-done(((bf16[4,192,512]{2,1,0:T(8,128)(2,1)}), bf16[4,192,512]{2,1,0:T(8,128)(2,1)S(1)}, u32[]{:S(2)}, u32[]{:S(2)}) %all-to-all-start.3) | async-done | bytes 786464 | tf_op jit(solution)/shard_map/all_to_all | solution.py:71
  152.8 5.6 %all-to-all-start.4 = ((bf16[4,192,512]{2,1,0:T(8,128)(2,1)}), bf16[4,192,512]{2,1,0:T(8,128)(2,1)}, u32[]{:S(2)}, u32[]{:S(2)}) async-start(bf16[4,192,512]{2,1,0:T(8,128)(2,1)} %bitcast.32), calls=%async_computation.4 | async-start | bytes 1572864 | tf_op jit(solution)/shard_map/all_to_all | solution.py:72
  158.4 0.6 copy.61
  159.0 1.2 reshape.163
  160.2 1.3 copy.62
  161.6 2.4 gather_fusion.2
  163.9 2.4 fusion.11
  166.3 6.5 %fusion.16 = f32[192,32,128]{2,1,0:T(8,128)} fusion(f32[192,48,128]{2,0,1:T(8,128)S(1)} %fusion.11, s32[48]{0:T(128)S(1)} %bitcast.113), kind=kOutput, calls=%fused_computation.20 | convolution fusion | flops 452986368 | bytes 7864512 | tf_op jit(solution)/shard_map/fkj,kc->fcj/dot_general | solution.py:79
  172.9 5.0 %copy.71 = f32[192,32,128]{0,2,1:T(8,128)} copy(f32[192,32,128]{2,1,0:T(8,128)} %fusion.16) | data formatting | bytes 6291456 | tf_op jit(solution)/shard_map/reshape | solution.py:80
  177.9 1.3 convert_bitcast_fusion
  179.2 1.8 copy.66
  181.0 5.3 %fusion.38 = (f32[192,2048]{0,1:T(8,128)}, f32[192,2048]{0,1:T(8,128)}) fusion(f32[192,4096]{0,1:T(8,128)} %bitcast.97, f32[192,4,512]{0,2,1:T(8,128)} %copy.66), kind=kLoop, calls=%fused_computation.56 | loop fusion | flops 393216 | bytes 7864320 | tf_op jit(solution)/shard_map/slice | solution.py:81
  186.3 7.1 %all-to-all-start.5 = ((f32[192,64,32]{0,2,1:T(8,128)}), f32[192,64,32]{0,2,1:T(8,128)}, u32[]{:S(2)}, u32[]{:S(2)}) async-start(f32[192,64,32]{0,2,1:T(8,128)} %bitcast.98), calls=%async_computation.5 | async-start | bytes 4194304 | tf_op jit(solution)/shard_map/all_to_all | solution.py:82
  193.4 0.3 all-reduce.3.cloned.1.call-start
  193.7 0.0 reduce-scatter.3.cloned.1.call-done
  193.7 21.2 %reduce-scatter.5.cloned.1.call-done = f32[192,1024]{1,0:T(8,128)} async-done(((f32[768,1024]{1,0:T(8,128)}), f32[192,1024]{1,0:T(8,128)}) %reduce-scatter.5.cloned.1.call-update) | async-done | bytes 786448 | tf_op jit(solution)/shard_map/reduce_scatter | solution.py:61
  215.0 29.5 %all-to-all-done.5 = f32[192,64,32]{0,2,1:T(8,128)} async-done(((f32[192,64,32]{0,2,1:T(8,128)}), f32[192,64,32]{0,2,1:T(8,128)}, u32[]{:S(2)}, u32[]{:S(2)}) %all-to-all-start.5) | async-done | bytes 1572896 | tf_op jit(solution)/shard_map/all_to_all | solution.py:82
  244.4 3.2 broadcast_select_fusion
  247.7 14.9 %scatter_fusion = f32[192,2048]{0,1:T(8,128)} fusion(f32[192,2048]{0,1:T(8,128)} %get-tuple-element.23, s32[2048]{0:T(1024)S(1)} %bitcast.111, f32[2048,192]{1,0:T(8,128)} %bitcast.100), kind=kCustom, calls=%fused_computation.3 | custom fusion | flops 393216 | bytes 4726784 | tf_op jit(solution)/shard_map/scatter-add | solution.py:85
  262.5 1.7 convert_bitcast_fusion.1
  264.2 1.2 copy.69
  265.5 145.1 %all-reduce.3.cloned.1.call-done = (f32[192,1024]{1,0:T(8,128)}, f32[192,1024]{1,0:T(8,128)}) async-done(((f32[192,1024]{1,0:T(8,128)}, f32[192,1024]{1,0:T(8,128)}), (f32[192,1024]{1,0:T(8,128)}, f32[192,1024]{1,0:T(8,128)})) %all-reduce.3.cloned.1.call-update) | async-done | bytes 1572880 | tf_op jit(solution)/shard_map/psum | solution.py:63
  410.6 2.8 broadcast_multiply_fusion
  (27 shorter events, 0.1 us)
Async XLA Ops:
  7.2 61.8 %copy-start = (bf16[1,48,128,128]{3,2,1,0:T(8,128)(2,1)S(1)}, bf16[1,48,128,128]{3,2,1,0:T(8,128)(2,1)}, u32[]{:S(2)}) copy-start(bf16[1,48,128,128]{3,2,1,0:T(8,128)(2,1)} %param.10) | copy-start | bytes 4718596
  7.2 94.0 %all-gather.3.cloned.1.call-start = ((), (), s32[]{:S(2)}) async-start(), calls=%async_computation.8 | async-start | bytes 1966080 | tf_op jit(solution)/shard_map/all_gather | solution.py:38
  11.1 9.1 %copy-start.7 = (s32[1,64]{1,0:T(1,128)S(1)}, s32[1,64]{1,0:T(1,128)}, u32[]{:S(2)}) copy-start(s32[1,64]{1,0:T(1,128)} %param.14) | copy-start | bytes 772
  20.2 16.2 %copy-start.6 = (s32[1,48]{1,0:T(1,128)S(1)}, s32[1,48]{1,0:T(1,128)}, u32[]{:S(2)}) copy-start(s32[1,48]{1,0:T(1,128)} %param.12) | copy-start | bytes 580
  20.3 16.2 %copy-start.1 = (bf16[1,192,2048]{2,1,0:T(8,128)(2,1)S(1)}, bf16[1,192,2048]{2,1,0:T(8,128)(2,1)}, u32[]{:S(2)}) copy-start(bf16[1,192,2048]{2,1,0:T(8,128)(2,1)} %param.9) | copy-start | bytes 2359300
  23.7 40.1 %all-to-all-start = ((bf16[192,64,32]{0,2,1:T(8,128)(2,1)}), bf16[192,64,32]{0,2,1:T(8,128)(2,1)S(1)}, u32[]{:S(2)}, u32[]{:S(2)}) async-start(bf16[192,64,32]{0,2,1:T(8,128)(2,1)} %select_select_fusion), calls=%async_computation | async-start | bytes 2097152 | tf_op jit(solution)/shard_map/all_to_all | solution.py:22
  35.7 76.1 %all-gather.5.cloned.1.call-start = ((), (), s32[]{:S(2)}) async-start(), calls=%async_computation.9 | async-start | bytes 1966080 | tf_op jit(solution)/shard_map/all_gather | solution.py:39
  69.0 2.8 copy-start.5
  77.0 7.7 %copy-start.2 = (bf16[1,192,2048]{2,1,0:T(8,128)(2,1)S(1)}, bf16[1,192,2048]{2,1,0:T(8,128)(2,1)}, u32[]{:S(2)}) copy-start(bf16[1,192,2048]{2,1,0:T(8,128)(2,1)} %param.9) | copy-start | bytes 2359300
  79.9 16.3 %all-to-all-start.1 = ((bf16[192,4,512]{2,0,1:T(8,128)(2,1)}), bf16[192,4,512]{2,0,1:T(8,128)(2,1)S(1)}, u32[]{:S(2)}, u32[]{:S(2)}) async-start(bf16[192,4,512]{2,0,1:T(8,128)(2,1)} %copy.58), calls=%async_computation.1 | async-start | bytes 1572864 | tf_op jit(solution)/shard_map/all_to_all | solution.py:42
  96.2 15.5 %all-to-all-start.2 = ((bf16[192,4,512]{2,0,1:T(8,128)(2,1)}), bf16[192,4,512]{2,0,1:T(8,128)(2,1)S(1)}, u32[]{:S(2)}, u32[]{:S(2)}) async-start(bf16[192,4,512]{2,0,1:T(8,128)(2,1)} %copy.59), calls=%async_computation.2 | async-start | bytes 1572864 | tf_op jit(solution)/shard_map/all_to_all | solution.py:43
  101.1 92.6 %reduce-scatter.3.cloned.1.call-start = ((), (), s32[]{:S(2)}) async-start(), calls=%async_computation.10 | async-start | bytes 3932160 | tf_op jit(solution)/shard_map/reduce_scatter | solution.py:60
  116.8 1.0 copy-start.3
  120.5 1.2 copy-start.4
  120.5 94.4 %reduce-scatter.5.cloned.1.call-start = ((), (), s32[]{:S(2)}) async-start(), calls=%async_computation.11 | async-start | bytes 3932160 | tf_op jit(solution)/shard_map/reduce_scatter | solution.py:61
  128.1 24.7 %all-to-all-start.3 = ((bf16[4,192,512]{2,1,0:T(8,128)(2,1)}), bf16[4,192,512]{2,1,0:T(8,128)(2,1)S(1)}, u32[]{:S(2)}, u32[]{:S(2)}) async-start(bf16[4,192,512]{2,1,0:T(8,128)(2,1)} %bitcast.108), calls=%async_computation.3 | async-start | bytes 1572864 | tf_op jit(solution)/shard_map/all_to_all | solution.py:71
  152.8 25.1 %all-to-all-start.4 = ((bf16[4,192,512]{2,1,0:T(8,128)(2,1)}), bf16[4,192,512]{2,1,0:T(8,128)(2,1)}, u32[]{:S(2)}, u32[]{:S(2)}) async-start(bf16[4,192,512]{2,1,0:T(8,128)(2,1)} %bitcast.32), calls=%async_computation.4 | async-start | bytes 1572864 | tf_op jit(solution)/shard_map/all_to_all | solution.py:72
  186.3 58.1 %all-to-all-start.5 = ((f32[192,64,32]{0,2,1:T(8,128)}), f32[192,64,32]{0,2,1:T(8,128)}, u32[]{:S(2)}, u32[]{:S(2)}) async-start(f32[192,64,32]{0,2,1:T(8,128)} %bitcast.98), calls=%async_computation.5 | async-start | bytes 4194304 | tf_op jit(solution)/shard_map/all_to_all | solution.py:82
  193.4 217.2 %all-reduce.3.cloned.1.call-start = ((), (), s32[]{:S(2)}) async-start(), calls=%async_computation.12 | async-start | bytes 3145728 | tf_op jit(solution)/shard_map/psum | solution.py:63
Sparse Core Ops, SparseCore 0:
  9.8 30.9 all-gather.2
  42.6 29.1 all-gather.4
  120.7 48.8 reduce-scatter.2
  172.0 42.9 reduce-scatter.4
  218.3 192.2 all-reduce.2
where the time goes:
time: 421 us; the launch traced here: 420 us
  waiting for transfers between devices  252 us (60%)
  local copies, waits for them, and re-layouts  41.9 us (10%)
  starting transfers between devices  39.8 us (9%)
  matrix products  37 us (9%)
  other arithmetic  35 us (8%)
  between operations  13.9 us (3%)
    psum x1, waiting for transfers between devices, per_device(): total_neigh, total_self = lax.psum((share_neigh, share_self), 'node')  145 us
    all_to_all x1, waiting for transfers between devices, per_device(): lax.all_to_all(outgoing, 'node', split_axis=1, concat_axis=1, tiled=True)  29.5 us
    all_to_all x1, waiting for transfers between devices, per_device(): lax.all_to_all(picked, 'node', split_axis=1, concat_axis=1, tiled=True)  26.1 us
    reduce_scatter x1, waiting for transfers between devices, per_device(): lax.psum_scatter(term_self, 'feat', scatter_dimension=0, tiled=True)  21.2 us
    scatter-add x1, other arithmetic, per_device(): grad_cols.at[:, targets.reshape(-1)]  14.9 us
    all_to_all x1, waiting for transfers between devices, per_device(): lax.all_to_all(back_agg, 'feat', split_axis=0, concat_axis=1, tiled=True)  14.1 us
    all_to_all x1, starting transfers between devices, per_device(): lax.all_to_all(picked, 'node', split_axis=1, concat_axis=1, tiled=True)  11.9 us
    gather x1, local copies, waits for them, and re-layouts, per_device(): jnp.take(own_cols, targets.reshape(-1), axis=1)  9.06 us
  transfers between devices with their start and end apart: 11, of which 7 were waited for; matrix products, arithmetic and copies ran while one was open for 24% of the time, Pallas kernels for 0%

commit v1 on v0

--- a/solution.py
+++ b/solution.py
@@ -79,7 +79,10 @@
     grad_ext = jnp.einsum("fkj,kc->fcj", spread, col_onehot, precision=lax.Precision.HIGHEST)
     grad_ext = grad_ext.reshape(feat_dev, col_blocks * tile_side)
     outgoing = grad_ext[:, own_rows:].reshape(feat_dev, parts, slots)
-    returned = lax.all_to_all(outgoing, "node", split_axis=1, concat_axis=1, tiled=True)
+    returned = jnp.concatenate(
+        lax.all_to_all(jnp.stack(jnp.split(outgoing, lax.axis_size("node"), axis=1)), "node", 0, 0),
+        axis=1,
+    )
     returned = jnp.where(live_slots[None], returned, jnp.zeros((), returned.dtype))
     grad_cols = grad_ext[:, :own_rows] + grad_own.astype(jnp.float32)
     grad_cols = grad_cols.at[:, targets.reshape(-1)].add(returned.reshape(feat_dev, parts * slots))

time: 421 us -> 443 us (1.052)
  local copies, waits for them, and re-layouts: 41.9 us -> 80.9 us
  waiting for transfers between devices: 252 us -> 235 us
    unnamed x20 -> x87, local copies, waits for them, and re-layouts: 5.82 us -> 43.7 us
    all_to_all x1, waiting for transfers between devices: 29.5 us -> 53 us  [per_device(): lax.all_to_all(jnp.stack(jnp.split(outgoing, lax.axis_size('node'), axis=...]
    reduce_scatter x1, waiting for transfers between devices: 21.2 us -> 0.02 us  [per_device(): lax.psum_scatter(term_self, 'feat', scatter_dimension=0, tiled=True)]
    psum x1, waiting for transfers between devices: 145 us -> 128 us  [per_device(): total_neigh, total_self = lax.psum((share_neigh, share_self), 'node')]
  transfers between devices with their start and end apart: 11 -> 11, of which waited for: 7 -> 6; matrix products, arithmetic and copies ran while one was open for 24% -> 31% of each run, Pallas kernels for 0% -> 0%
where the time goes in v1:
time: 443 us; the launch traced here: 442 us
  waiting for transfers between devices  235 us (53%)
  local copies, waits for them, and re-layouts  80.9 us (18%)
  starting transfers between devices  40.3 us (9%)
  matrix products  37.9 us (9%)
  other arithmetic  34.1 us (8%)
  between operations  14 us (3%)
    psum x1, waiting for transfers between devices, per_device(): total_neigh, total_self = lax.psum((share_neigh, share_self), 'node')  128 us
    all_to_all x1, waiting for transfers between devices, per_device(): lax.all_to_all(jnp.stack(jnp.split(outgoing, lax.axis_size('node'), axis=...  53 us
    unnamed x87, local copies, waits for them, and re-layouts  43.7 us
    all_to_all x1, waiting for transfers between devices, per_device(): lax.all_to_all(picked, 'node', split_axis=1, concat_axis=1, tiled=True)  26.1 us
    scatter-add x1, other arithmetic, per_device(): grad_cols.at[:, targets.reshape(-1)]  15 us
    all_to_all x1, starting transfers between devices, per_device(): lax.all_to_all(picked, 'node', split_axis=1, concat_axis=1, tiled=True)  11.9 us
    all_to_all x1, waiting for transfers between devices, per_device(): lax.all_to_all(back_agg, 'feat', split_axis=0, concat_axis=1, tiled=True)  11.5 us
    gather x1, local copies, waits for them, and re-layouts, per_device(): jnp.take(own_cols, targets.reshape(-1), axis=1)  9.06 us
  transfers between devices with their start and end apart: 11, of which 6 were waited for; matrix products, arithmetic and copies ran while one was open for 31% of the time, Pallas kernels for 0%

profile of v1, /device:TPU:8, one launch (start us, length us, event | category | flops | bytes accessed | tf_op | source)
XLA Modules:
  0.0 442.2 jit_solution(13668486838258660233)
XLA Ops:
  7.2 0.7 all-gather.3.cloned.1.call-update
  7.9 1.4 copy.116
  9.7 9.1 %gather_fusion = bf16[2048,192]{1,0:T(8,128)(2,1)} fusion(bf16[192,2048]{0,1:T(8,128)(2,1)S(1)} %bitcast.358, s32[2048]{0:T(1024)S(1)} %broadcast_clamp_fusion), kind=kCustom, calls=%fused_computation | custom fusion | bytes 1581056 | tf_op jit(solution)/shard_map/jit(_take)/gather | solution.py:20
  18.9 3.4 select_select_fusion
  22.3 11.9 %all-to-all-start = ((bf16[192,64,32]{0,2,1:T(8,128)(2,1)}), bf16[192,64,32]{0,2,1:T(8,128)(2,1)S(1)}, u32[]{:S(2)}, u32[]{:S(2)}) async-start(bf16[192,64,32]{0,2,1:T(8,128)(2,1)} %select_select_fusion), calls=%async_computation | async-start | bytes 2097152 | tf_op jit(solution)/shard_map/all_to_all | solution.py:22
  34.3 0.7 all-gather.5.cloned.1.call-update
  35.2 1.1 copy.118
  36.3 26.1 %all-to-all-done = bf16[192,64,32]{0,2,1:T(8,128)(2,1)S(1)} async-done(((bf16[192,64,32]{0,2,1:T(8,128)(2,1)}), bf16[192,64,32]{0,2,1:T(8,128)(2,1)S(1)}, u32[]{:S(2)}, u32[]{:S(2)}) %all-to-all-start) | async-done | bytes 786464 | tf_op jit(solution)/shard_map/all_to_all | solution.py:22
  62.4 1.2 copy.119
  63.7 1.5 pad_maximum_fusion
  65.2 2.4 gather_fusion.1
  67.6 2.8 fusion.8
  70.4 5.2 %fusion.28 = bf16[192,16,128]{2,1,0:T(8,128)(2,1)} fusion(f32[192,48,128]{2,0,1:T(8,128)S(1)} %fusion.8, s32[48]{0:T(128)S(1)} %bitcast.437), kind=kOutput, calls=%fused_computation.35 | convolution fusion | flops 226886400 | bytes 5505216 | tf_op jit(solution)/shard_map/fki,kr->fri/dot_general | solution.py:33
  75.6 1.8 convert_element_type.50
  77.4 1.0 copy.121
  78.4 4.9 %all-to-all-start.1 = ((bf16[192,4,512]{2,0,1:T(8,128)(2,1)}), bf16[192,4,512]{2,0,1:T(8,128)(2,1)S(1)}, u32[]{:S(2)}, u32[]{:S(2)}) async-start(bf16[192,4,512]{2,0,1:T(8,128)(2,1)} %copy.121), calls=%async_computation.1 | async-start | bytes 1572864 | tf_op jit(solution)/shard_map/all_to_all | solution.py:42
  83.4 1.4 all_to_all.58
  84.8 2.2 copy.122
  87.0 7.8 %all-to-all-done.1 = bf16[192,4,512]{2,0,1:T(8,128)(2,1)S(1)} async-done(((bf16[192,4,512]{2,0,1:T(8,128)(2,1)}), bf16[192,4,512]{2,0,1:T(8,128)(2,1)S(1)}, u32[]{:S(2)}, u32[]{:S(2)}) %all-to-all-start.1) | async-done | bytes 786464 | tf_op jit(solution)/shard_map/all_to_all | solution.py:42
  94.8 4.9 %all-to-all-start.2 = ((bf16[192,4,512]{2,0,1:T(8,128)(2,1)}), bf16[192,4,512]{2,0,1:T(8,128)(2,1)S(1)}, u32[]{:S(2)}, u32[]{:S(2)}) async-start(bf16[192,4,512]{2,0,1:T(8,128)(2,1)} %copy.122), calls=%async_computation.2 | async-start | bytes 1572864 | tf_op jit(solution)/shard_map/all_to_all | solution.py:43
  99.7 3.8 fusion.41
  103.5 6.8 %all-to-all-done.2 = bf16[192,4,512]{2,0,1:T(8,128)(2,1)S(1)} async-done(((bf16[192,4,512]{2,0,1:T(8,128)(2,1)}), bf16[192,4,512]{2,0,1:T(8,128)(2,1)S(1)}, u32[]{:S(2)}, u32[]{:S(2)}) %all-to-all-start.2) | async-done | bytes 786464 | tf_op jit(solution)/shard_map/all_to_all | solution.py:43
  110.3 5.1 %fusion.15 = (bf16[512,1024]{1,0:T(8,128)(2,1)S(1)}, bf16[1,512,1024]{2,1,0:T(8,128)(2,1)}) fusion(bf16[1,512,1024]{2,1,0:T(8,128)(2,1)} %param.17, f32[512,1024]{1,0:T(8,128)} %fusion.41, bf16[768,512]{1,0:T(8,128)(2,1)S(1)} %bitcast.425, bf16[768,1024]{1,0:T(8,128)(2,1)} %all-gather.5.cloned.1.call-done), kind=kOutput, calls=%fused_computation.18 | convolution fusion | flops 812122112 | bytes 7602176 | tf_op jit(solution)/shard_map/dot_general | solution.py:47
  115.4 1.0 copy-done.3
  116.4 2.7 fusion.42
  119.1 1.2 copy-done.4
  120.3 3.3 fusion.26
  123.6 2.3 copy.123
  125.9 5.6 %all-to-all-start.3 = ((bf16[4,192,512]{2,1,0:T(8,128)(2,1)}), bf16[4,192,512]{2,1,0:T(8,128)(2,1)}, u32[]{:S(2)}, u32[]{:S(2)}) async-start(bf16[4,192,512]{2,1,0:T(8,128)(2,1)} %bitcast.431), calls=%async_computation.3 | async-start | bytes 1572864 | tf_op jit(solution)/shard_map/all_to_all | solution.py:71
  131.5 3.3 fusion.27
  134.9 2.3 copy.128
  137.2 2.7 convolution_bitcast_fusion
  139.9 11.5 %all-to-all-done.3 = bf16[4,192,512]{2,1,0:T(8,128)(2,1)} async-done(((bf16[4,192,512]{2,1,0:T(8,128)(2,1)}), bf16[4,192,512]{2,1,0:T(8,128)(2,1)}, u32[]{:S(2)}, u32[]{:S(2)}) %all-to-all-start.3) | async-done | bytes 786464 | tf_op jit(solution)/shard_map/all_to_all | solution.py:71
  151.4 5.6 %all-to-all-start.4 = ((bf16[4,192,512]{2,1,0:T(8,128)(2,1)}), bf16[4,192,512]{2,1,0:T(8,128)(2,1)}, u32[]{:S(2)}, u32[]{:S(2)}) async-start(bf16[4,192,512]{2,1,0:T(8,128)(2,1)} %bitcast.32), calls=%async_computation.4 | async-start | bytes 1572864 | tf_op jit(solution)/shard_map/all_to_all | solution.py:72
  157.1 1.8 copy.124
  159.3 2.4 gather_fusion.2
  161.7 2.4 fusion.11
  164.1 6.5 %fusion.18 = f32[192,32,128]{2,1,0:T(8,128)} fusion(f32[192,48,128]{2,0,1:T(8,128)S(1)} %fusion.11, s32[48]{0:T(128)S(1)} %bitcast.438), kind=kOutput, calls=%fused_computation.23 | convolution fusion | flops 452986368 | bytes 7864512 | tf_op jit(solution)/shard_map/fkj,kc->fcj/dot_general | solution.py:79
  170.7 5.0 %copy.134 = f32[192,32,128]{0,2,1:T(8,128)} copy(f32[192,32,128]{2,1,0:T(8,128)} %fusion.18) | data formatting | bytes 6291456 | tf_op jit(solution)/shard_map/reshape | solution.py:80
  175.6 1.3 convert_bitcast_fusion
  177.0 1.8 copy.129
  178.8 4.6 %fusion.40 = (f32[192,2048]{0,1:T(8,128)S(1)}, f32[192,2048]{0,1:T(8,128)}) fusion(f32[192,4096]{0,1:T(8,128)} %bitcast.359, f32[192,4,512]{0,2,1:T(8,128)} %copy.129), kind=kLoop, calls=%fused_computation.186 | loop fusion | flops 393216 | bytes 7864320 | tf_op jit(solution)/shard_map/slice | solution.py:81
  187.7 0.6 constant_dynamic-update-slice_fusion.56
  192.0 0.6 constant_dynamic-update-slice_fusion.49
  196.3 0.6 constant_dynamic-update-slice_fusion.42
  201.1 0.6 constant_dynamic-update-slice_fusion.34
  203.6 0.6 constant_dynamic-update-slice_fusion.30
  204.2 0.6 constant_dynamic-update-slice_fusion.29
  206.1 0.6 constant_dynamic-update-slice_fusion.26
  211.0 0.6 constant_dynamic-update-slice_fusion.18
  213.4 0.6 constant_dynamic-update-slice_fusion.14
  218.9 0.6 constant_dynamic-update-slice_fusion.5
  220.8 0.6 constant_dynamic-update-slice_fusion.2
  221.4 0.6 constant_dynamic-update-slice_fusion.1
  222.0 0.6 constant_dynamic-update-slice_fusion
  222.6 7.0 %all-to-all-start.5 = ((f32[64,192,1,32]{1,3,2,0:T(8,128)}), f32[64,192,1,32]{1,3,2,0:T(8,128)}, u32[]{:S(2)}, u32[]{:S(2)}) async-start(f32[64,192,1,32]{1,3,2,0:T(8,128)} %constant_dynamic-update-slice_fusion), calls=%async_computation.5 | async-start | bytes 4194304 | tf_op jit(solution)/shard_map/all_to_all | solution.py:83
  230.2 53.0 %all-to-all-done.5 = f32[64,192,1,32]{1,3,2,0:T(8,128)} async-done(((f32[64,192,1,32]{1,3,2,0:T(8,128)}), f32[64,192,1,32]{1,3,2,0:T(8,128)}, u32[]{:S(2)}, u32[]{:S(2)}) %all-to-all-start.5) | async-done | bytes 1572896 | tf_op jit(solution)/shard_map/all_to_all | solution.py:83
  283.3 3.2 bitcast_select_fusion
  286.5 15.0 %scatter_custom_fusion = f32[192,2048]{0,1:T(8,128)} fusion(f32[192,2048]{0,1:T(8,128)} %get-tuple-element.23, s32[2048]{0:T(1024)S(1)} %bitcast.434, f32[192,2048]{0,1:T(8,128)} %bitcast_select_fusion), kind=kCustom, calls=%fused_computation.19 | custom fusion | flops 393216 | bytes 3670016 | tf_op jit(solution)/shard_map/scatter-add | solution.py:88
  301.5 1.7 convert_bitcast_fusion.1
  303.2 1.2 copy.132
  304.5 128.0 %all-reduce.3.cloned.1.call-done = (f32[192,1024]{1,0:T(8,128)}, f32[192,1024]{1,0:T(8,128)}) async-done(((f32[192,1024]{1,0:T(8,128)}, f32[192,1024]{1,0:T(8,128)}), (f32[192,1024]{1,0:T(8,128)}, f32[192,1024]{1,0:T(8,128)})) %all-reduce.3.cloned.1.call-update) | async-done | bytes 1572880 | tf_op jit(solution)/shard_map/psum | solution.py:63
  432.5 2.2 broadcast_multiply_fusion.1
  434.7 1.0 broadcast_multiply_fusion
  (100 shorter events, 32.9 us)
Async XLA Ops:
  7.2 60.4 %copy-start = (bf16[1,48,128,128]{3,2,1,0:T(8,128)(2,1)S(1)}, bf16[1,48,128,128]{3,2,1,0:T(8,128)(2,1)}, u32[]{:S(2)}) copy-start(bf16[1,48,128,128]{3,2,1,0:T(8,128)(2,1)} %param.10) | copy-start | bytes 4718596
  7.2 2.2 copy-start.6
  7.2 92.5 %all-gather.3.cloned.1.call-start = ((), (), s32[]{:S(2)}) async-start(), calls=%async_computation.8 | async-start | bytes 1966080 | tf_op jit(solution)/shard_map/all_gather | solution.py:38
  9.7 9.1 %copy-start.7 = (s32[1,64]{1,0:T(1,128)S(1)}, s32[1,64]{1,0:T(1,128)}, u32[]{:S(2)}) copy-start(s32[1,64]{1,0:T(1,128)} %param.14) | copy-start | bytes 772
  18.8 16.2 %copy-start.8 = (s32[1,48]{1,0:T(1,128)S(1)}, s32[1,48]{1,0:T(1,128)}, u32[]{:S(2)}) copy-start(s32[1,48]{1,0:T(1,128)} %param.11) | copy-start | bytes 580
  18.9 16.2 %copy-start.9 = (s32[1,48]{1,0:T(1,128)S(1)}, s32[1,48]{1,0:T(1,128)}, u32[]{:S(2)}) copy-start(s32[1,48]{1,0:T(1,128)} %param.12) | copy-start | bytes 580
  18.9 16.2 %copy-start.1 = (bf16[1,192,2048]{2,1,0:T(8,128)(2,1)S(1)}, bf16[1,192,2048]{2,1,0:T(8,128)(2,1)}, u32[]{:S(2)}) copy-start(bf16[1,192,2048]{2,1,0:T(8,128)(2,1)} %param.9) | copy-start | bytes 2359300
  22.3 40.1 %all-to-all-start = ((bf16[192,64,32]{0,2,1:T(8,128)(2,1)}), bf16[192,64,32]{0,2,1:T(8,128)(2,1)S(1)}, u32[]{:S(2)}, u32[]{:S(2)}) async-start(bf16[192,64,32]{0,2,1:T(8,128)(2,1)} %select_select_fusion), calls=%async_computation | async-start | bytes 2097152 | tf_op jit(solution)/shard_map/all_to_all | solution.py:22
  34.2 76.1 %all-gather.5.cloned.1.call-start = ((), (), s32[]{:S(2)}) async-start(), calls=%async_computation.9 | async-start | bytes 1966080 | tf_op jit(solution)/shard_map/all_gather | solution.py:39
  75.6 7.8 %copy-start.2 = (bf16[1,192,2048]{2,1,0:T(8,128)(2,1)S(1)}, bf16[1,192,2048]{2,1,0:T(8,128)(2,1)}, u32[]{:S(2)}) copy-start(bf16[1,192,2048]{2,1,0:T(8,128)(2,1)} %param.9) | copy-start | bytes 2359300
  78.4 16.3 %all-to-all-start.1 = ((bf16[192,4,512]{2,0,1:T(8,128)(2,1)}), bf16[192,4,512]{2,0,1:T(8,128)(2,1)S(1)}, u32[]{:S(2)}, u32[]{:S(2)}) async-start(bf16[192,4,512]{2,0,1:T(8,128)(2,1)} %copy.121), calls=%async_computation.1 | async-start | bytes 1572864 | tf_op jit(solution)/shard_map/all_to_all | solution.py:42
  94.8 15.5 %all-to-all-start.2 = ((bf16[192,4,512]{2,0,1:T(8,128)(2,1)}), bf16[192,4,512]{2,0,1:T(8,128)(2,1)S(1)}, u32[]{:S(2)}, u32[]{:S(2)}) async-start(bf16[192,4,512]{2,0,1:T(8,128)(2,1)} %copy.122), calls=%async_computation.2 | async-start | bytes 1572864 | tf_op jit(solution)/shard_map/all_to_all | solution.py:43
  99.7 130.5 %reduce-scatter.3.cloned.1.call-start = ((), (), s32[]{:S(2)}) async-start(), calls=%async_computation.10 | async-start | bytes 3932160 | tf_op jit(solution)/shard_map/reduce_scatter | solution.py:60
  115.4 1.0 copy-start.3
  119.1 1.2 copy-start.4
  125.9 25.5 %all-to-all-start.3 = ((bf16[4,192,512]{2,1,0:T(8,128)(2,1)}), bf16[4,192,512]{2,1,0:T(8,128)(2,1)}, u32[]{:S(2)}, u32[]{:S(2)}) async-start(bf16[4,192,512]{2,1,0:T(8,128)(2,1)} %bitcast.431), calls=%async_computation.3 | async-start | bytes 1572864 | tf_op jit(solution)/shard_map/all_to_all | solution.py:71
  131.5 98.7 %reduce-scatter.5.cloned.1.call-start = ((), (), s32[]{:S(2)}) async-start(), calls=%async_computation.11 | async-start | bytes 3932160 | tf_op jit(solution)/shard_map/reduce_scatter | solution.py:61
  151.4 24.2 %all-to-all-start.4 = ((bf16[4,192,512]{2,1,0:T(8,128)(2,1)}), bf16[4,192,512]{2,1,0:T(8,128)(2,1)}, u32[]{:S(2)}, u32[]{:S(2)}) async-start(bf16[4,192,512]{2,1,0:T(8,128)(2,1)} %bitcast.32), calls=%async_computation.4 | async-start | bytes 1572864 | tf_op jit(solution)/shard_map/all_to_all | solution.py:72
  222.6 60.6 %all-to-all-start.5 = ((f32[64,192,1,32]{1,3,2,0:T(8,128)}), f32[64,192,1,32]{1,3,2,0:T(8,128)}, u32[]{:S(2)}, u32[]{:S(2)}) async-start(f32[64,192,1,32]{1,3,2,0:T(8,128)} %constant_dynamic-update-slice_fusion), calls=%async_computation.5 | async-start | bytes 4194304 | tf_op jit(solution)/shard_map/all_to_all | solution.py:83
  229.6 202.9 %all-reduce.3.cloned.1.call-start = ((), (), s32[]{:S(2)}) async-start(), calls=%async_computation.12 | async-start | bytes 3145728 | tf_op jit(solution)/shard_map/psum | solution.py:63
  432.5 2.2 copy-start.5
Sparse Core Ops, SparseCore 0:
  9.8 30.9 all-gather.2
  42.6 29.1 all-gather.4
  119.2 48.6 reduce-scatter.2
  170.3 43.0 reduce-scatter.4
  233.6 198.8 all-reduce.2
